TPU v7x, 32 devices: a whole 2x2x4 slice. The times are simulated.
32 devices in a mesh: groups: 2 (over x), pop: 8 (over z, y), tensor: 2 (over core).
Axes of the slice: x: 2, y: 2, z: 4, core: 2. Of those that a mesh axis runs over, the one named last changes fastest.
Arguments:
- prompts: bfloat16 [48, 8192], P('groups'), parts along dimension 0, may hold values from -6 to 6
- gate_weight: bfloat16 [8192, 14848], P('pop', 'tensor'), may hold values from -0.0625 to 0.0625
- up_weight: bfloat16 [8192, 14848], P('pop', 'tensor'), may hold values from -0.0625 to 0.0625
- down_weight_matrix: bfloat16 [14848, 8192], P('tensor', 'pop'), may hold values from -0.046875 to 0.046875
- gate_in: bfloat16 [16, 8192, 4], P(('groups', 'pop')), parts along dimension 0, may hold values from -6 to 6
- gate_output_factors: bfloat16 [16, 14848, 4], P(('groups', 'pop'), 'tensor'), parts along dimension 0, may hold values from -6 to 6
- up_in: bfloat16 [16, 8192, 4], P(('groups', 'pop')), parts along dimension 0, may hold values from -6 to 6
- up_output_factors: bfloat16 [16, 14848, 4], P(('groups', 'pop'), 'tensor'), parts along dimension 0, may hold values from -6 to 6
- down_input_factors: bfloat16 [16, 14848, 4], P('groups', 'tensor'), parts along dimension 0, may hold values from -6 to 6
- down_out: bfloat16 [16, 8192, 4], P('groups', 'pop'), parts along dimension 0, may hold values from -6 to 6
- label_head: bfloat16 [8192, 128], P('tensor'), may hold values from -0.1875 to 0.1875
- targets: int32 [48], P('groups'), parts along dimension 0, may hold values from 0 to 127
Outputs:
- update: bfloat16 [29696, 8192], P(('groups', 'tensor'), 'pop'), parts along dimension 0
- scores: float32 [16], P(('groups', 'pop')), parts along dimension 0
There are 2 independent parts, one for each index of `groups`. A program takes and returns all parts, laid end to end along the dimension named above; an argument that names none is the same for every part. Nothing has to cross between parts.
All inputs are finite; a program needn't handle non-finite values.
Results may differ from a plain program's by a relative error of at most 0.023.
Values may be sent and summed in bfloat16 or wider, within the bound.
A program may use at most 256 MiB of HBM per device.

v0:
```python
import math

import jax
import jax.numpy as jnp
from jax import lax
from jax.sharding import PartitionSpec as P

noise_scale = 0.2
norm_eps = 1e-06


def scaled_rows(values):
    return values * lax.rsqrt(jnp.mean(values * values, axis=-1, keepdims=True) + norm_eps)


def build_hidden(
    gate_baseline, up_baseline, lowrank_gate, lowrank_up, gate_output_factors, up_output_factors
):
    gate_activation = gate_baseline.astype(jnp.float32)[None] + jnp.einsum(
        "hvw,hpw->hvp", lowrank_gate, gate_output_factors, preferred_element_type=jnp.float32
    )
    upper_bound = up_baseline.astype(jnp.float32)[None] + jnp.einsum(
        "hvw,hpw->hvp", lowrank_up, up_output_factors, preferred_element_type=jnp.float32
    )
    return (jax.nn.silu(gate_activation) * upper_bound).astype(jnp.bfloat16)


def label_terms(logits, targets):
    labels = logits.shape[1]
    picks = targets[:, None] == jnp.arange(labels, dtype=jnp.int32)[None, :]
    picked = jnp.sum(jnp.where(picks, logits, 0.0), axis=1)
    return picked - jnp.log(jnp.sum(jnp.exp(logits), axis=1))


def body(
    prompts,
    gate_weight,
    up_weight,
    down_weight_matrix,
    gate_in,
    gate_output_factors,
    up_in,
    up_output_factors,
    down_input_factors,
    down_out,
    label_head,
    targets,
):
    member = lax.axis_index("pop")
    width = prompts.shape[1]
    in_block = gate_weight.shape[0]
    ffn_half = gate_output_factors.shape[1]
    total_ff = ffn_half * lax.axis_size("tensor")
    members = down_input_factors.shape[0]
    rank = down_input_factors.shape[2]
    prompt_f = prompts.astype(jnp.float32)
    normed = scaled_rows(prompt_f).astype(jnp.bfloat16)
    own_cols = lax.dynamic_slice_in_dim(normed, member * in_block, in_block, 1)
    part_gate = jnp.dot(own_cols, gate_weight, preferred_element_type=jnp.float32)
    part_up = jnp.dot(own_cols, up_weight, preferred_element_type=jnp.float32)
    total_gate, total_up = lax.psum((part_gate, part_up), "pop")
    gate_baseline = total_gate.astype(jnp.bfloat16)
    up_baseline = total_up.astype(jnp.bfloat16)
    in_scale = noise_scale / math.sqrt(width)
    lowrank_gate = (
        in_scale * jnp.einsum("rd,mdk->mrk", normed, gate_in, preferred_element_type=jnp.float32)
    ).astype(jnp.bfloat16)
    lowrank_up = (
        in_scale * jnp.einsum("rd,mdk->mrk", normed, up_in, preferred_element_type=jnp.float32)
    ).astype(jnp.bfloat16)
    down_scale = noise_scale / math.sqrt(total_ff)
    hidden_state = build_hidden(
        gate_baseline, up_baseline, lowrank_gate, lowrank_up, gate_output_factors, up_output_factors
    )
    hidden_portion = lax.all_gather(hidden_state, "pop", axis=0, tiled=True)
    out_piece = down_out.astype(jnp.float32)
    entry_point = jnp.einsum(
        "uaz,zh->uah", hidden_portion, down_weight_matrix, preferred_element_type=jnp.float32
    )
    low_part = down_scale * jnp.einsum(
        "lpq,lqb->lpb", hidden_portion, down_input_factors, preferred_element_type=jnp.float32
    )
    partial_rows = entry_point + jnp.einsum(
        "mrk,mdk->mrd", low_part, out_piece, precision=lax.Precision.HIGHEST
    )
    rows_here = lax.all_to_all(partial_rows, "pop", split_axis=0, concat_axis=2, tiled=True)
    summed = lax.psum(rows_here, "tensor")[0]
    output = prompt_f + summed
    final = scaled_rows(output).astype(jnp.bfloat16)
    half = label_head.shape[0]
    own_half = lax.dynamic_slice_in_dim(final, lax.axis_index("tensor") * half, half, 1)
    logits = lax.psum(jnp.dot(own_half, label_head, preferred_element_type=jnp.float32), "tensor")
    reward = jnp.mean(label_terms(logits, targets))
    rewards = lax.all_gather(reward.reshape(1), "pop", axis=0, tiled=True)
    centre = jnp.mean(rewards)
    spread = jnp.mean((rewards - centre) * (rewards - centre))
    scores = (rewards - centre) * lax.rsqrt(spread + norm_eps)
    weighted = (scores[:, None, None] * down_out.astype(jnp.float32)).astype(jnp.bfloat16)
    update = jnp.einsum(
        "mfk,mdk->fd", down_input_factors, weighted, preferred_element_type=jnp.float32
    ) * (1.0 / math.sqrt(members * rank))
    own_score = lax.dynamic_slice_in_dim(scores, member, 1, 0)
    return (update.astype(jnp.bfloat16), own_score)


def solution(mesh):
    placed = (
        P("groups", None),
        P("pop", "tensor"),
        P("pop", "tensor"),
        P("tensor", "pop"),
        P(("groups", "pop"), None, None),
        P(("groups", "pop"), "tensor", None),
        P(("groups", "pop"), None, None),
        P(("groups", "pop"), "tensor", None),
        P("groups", "tensor", None),
        P("groups", "pop", None),
        P("tensor", None),
        P("groups"),
    )
    return jax.shard_map(
        body,
        mesh=mesh,
        in_specs=placed,
        out_specs=(P(("groups", "tensor"), "pop"), P(("groups", "pop"))),
        check_vma=False,
    )
```

profile of v0, /device:TPU:0, one launch (start us, length us, event | category | flops | bytes accessed | tf_op | source)
XLA Modules:
  0.0 282.1 jit_solution(8416717195286552256)
XLA Ops:
  7.2 0.0 copy-start
  7.2 0.0 all-gather.3.cloned.1.call-start
  7.2 1.3 fusion.8
  8.5 1.1 fusion.9
  9.6 0.0 copy-start.2
  9.7 7.6 %fusion.21 = f32[24,7424]{1,0:T(8,128)S(1)} fusion(bf16[1024,7424]{1,0:T(8,128)(2,1)} %param.14, bf16[24,8192]{1,0:T(8,128)(2,1)S(1)} %fusion.9, s32[]{:T(128)S(6)} %select_n.13), kind=kOutput, calls=%fused_computation.31 | convolution fusion | flops 364904448 | bytes 15966212 | tf_op jit(solution)/shard_map/dot_general | solution.py:60
  17.2 2.1 copy-done.2
  19.3 0.0 copy-start.4
  19.3 2.1 fusion.23
  21.4 80.8 %all-reduce.6 = (bf16[24,7424]{1,0:T(8,128)(2,1)S(1)}, bf16[24,7424]{1,0:T(8,128)(2,1)}) all-reduce(f32[24,7424]{1,0:T(8,128)S(1)} %fusion.23, f32[24,7424]{1,0:T(8,128)S(1)} %fusion.21), channel_id=1, replica_groups=mesh['groups'=2,'pop'=8,'tensor'=2] {'pop'}, use_global_device_ids=true, to_apply=%region_1.0 | all-reduce | flops 356352 | bytes 2138112 | tf_op jit(solution)/shard_map/psum | solution.py:61
  102.2 0.0 copy-done.4
  102.2 0.0 copy-done.6
  102.2 0.7 convolution_add_fusion.1
  102.8 0.0 copy-done.9
  102.9 0.0 copy-done.10
  102.9 2.4 fusion.5
  105.3 0.0 all-gather.3.cloned.1.call-update
  105.3 0.0 all-reduce.5.cloned.1.call-start
  105.3 56.4 %all-gather.3.cloned.1.call-done = bf16[192,7424]{1,0:T(8,128)(2,1)} async-done(((bf16[24,7424]{1,0:T(8,128)(2,1)}), bf16[192,7424]{1,0:T(8,128)(2,1)}) %all-gather.3.cloned.1.call-update) | async-done | bytes 2850832 | tf_op jit(solution)/shard_map/all_gather | solution.py:75
  161.8 2.8 convolution_multiply_fusion
  164.6 0.0 copy-start.7
  164.6 0.0 copy-start.8
  164.6 7.9 %fusion.1 = f32[8,24,1024]{2,1,0:T(8,128)S(1)} fusion(bf16[8,24,7424]{2,1,0:T(8,128)(2,1)} %bitcast.50, bf16[7424,1024]{1,0:T(8,128)(2,1)} %param.15), kind=kOutput, calls=%fused_computation.2 | convolution fusion | flops 2919235584 | bytes 18841600 | tf_op jit(solution)/shard_map/uaz,zh->uah/dot_general | solution.py:77
  172.6 0.0 copy-done.5
  172.6 0.6 convolution_add_fusion.2
  173.1 22.9 %all_to_all.18 = f32[8,24,1024]{2,1,0:T(8,128)S(1)} all-to-all(f32[8,24,1024]{2,1,0:T(8,128)S(1)} %convolution_add_fusion.2), channel_id=1, replica_groups=mesh['groups'=2,'pop'=8,'tensor'=2] {'pop'}, dimensions={0} | all-to-all | bytes 1572864 | tf_op jit(solution)/shard_map/all_to_all | solution.py:86
  196.0 0.9 copy.23
  197.0 0.0 all-reduce.5.cloned.1.call-update
  197.0 0.0 copy-done.11
  197.0 0.6 dynamic-slice
  197.7 17.0 %all-reduce.5.cloned.1.call-done = f32[24,8192]{1,0:T(8,128)} async-done(((f32[24,8192]{1,0:T(8,128)}), f32[24,8192]{1,0:T(8,128)}) %all-reduce.5.cloned.1.call-update) | async-done | bytes 786448 | tf_op jit(solution)/shard_map/psum | solution.py:87
  214.6 0.0 copy-done.3
  214.6 1.4 multiply_reduce_fusion
  216.0 0.0 copy-done
  216.0 0.3 fusion.11
  216.3 3.4 %psum.31 = f32[24,128]{1,0:T(8,128)S(1)} all-reduce(f32[24,128]{1,0:T(8,128)S(1)} %fusion.11), channel_id=1, replica_groups=mesh['groups'=2,'pop'=8,'tensor'=2] {'tensor'}, use_global_device_ids=true, to_apply=%region_5.6 | all-reduce | flops 3072 | bytes 24576 | tf_op jit(solution)/shard_map/psum | solution.py:92
  219.7 0.0 copy-done.7
  219.7 0.2 exponential_reduce_fusion
  219.9 0.6 subtract_reduce_fusion
  221.2 0.7 dynamic-update-slice
  221.9 21.8 %all-reduce = f32[8]{0:T(128)S(1)} all-reduce(f32[8]{0:T(128)S(1)} %dynamic-update-slice), channel_id=1, replica_groups=mesh['groups'=2,'pop'=8,'tensor'=2] {'pop'}, use_global_device_ids=true, to_apply=%add | all-reduce | flops 8 | bytes 64
  243.7 0.6 reduce_sum.68
  245.0 0.6 multiply_reduce_fusion.1
  246.3 0.0 copy-done.8
  246.3 8.0 %fusion.3 = bf16[7424,1024]{0,1:T(8,128)(2,1)} fusion(bf16[8,7424,4]{1,2,0:T(4,128)(2,1)S(1)} %copy-done.8, bf16[8,1024,4]{1,2,0:T(4,128)(2,1)S(1)} %copy-done.5, f32[8]{0:T(128)S(1)} %subtract_multiply_fusion), kind=kOutput, calls=%fused_computation.4 | convolution fusion | flops 501841920 | bytes 15745056 | tf_op jit(solution)/shard_map/mfk,mdk->fd/dot_general | solution.py:99
  254.3 0.6 dynamic_slice.11
  254.9 20.4 %copy.20 = bf16[7424,1024]{1,0:T(8,128)(2,1)} copy(bf16[7424,1024]{0,1:T(8,128)(2,1)} %fusion.3) | data formatting | bytes 30408704
  275.3 0.0 copy-done.1
  (11 shorter events, 0.0 us)
Async XLA Ops:
  7.2 208.8 %copy-start = (bf16[4096,128]{1,0:T(8,128)(2,1)S(1)}, bf16[4096,128]{1,0:T(8,128)(2,1)}, u32[]{:S(2)}) copy-start(bf16[4096,128]{1,0:T(8,128)(2,1)} %param.22) | copy-start | bytes 3145732
  7.2 154.6 %all-gather.3.cloned.1.call-start = ((), (), s32[]{:S(2)}) async-start(), calls=%async_computation.2 | async-start | bytes 3207168 | tf_op jit(solution)/shard_map/all_gather | solution.py:75
  9.6 9.7 %copy-start.2 = (bf16[1024,7424]{1,0:T(8,128)(2,1)S(1)}, bf16[1024,7424]{1,0:T(8,128)(2,1)}, u32[]{:S(2)}) copy-start(bf16[1024,7424]{1,0:T(8,128)(2,1)} %param.13) | copy-start | bytes 45613060
  19.3 82.9 %copy-start.4 = (bf16[1,8192,4]{1,2,0:T(4,128)(2,1)S(1)}, bf16[1,8192,4]{1,2,0:T(4,128)(2,1)}, u32[]{:S(2)}) copy-start(bf16[1,8192,4]{1,2,0:T(4,128)(2,1)} %param.16) | copy-start | bytes 196612
  19.3 82.9 %copy-start.6 = (bf16[1,7424,4]{1,2,0:T(4,128)(2,1)S(1)}, bf16[1,7424,4]{1,2,0:T(4,128)(2,1)}, u32[]{:S(2)}) copy-start(bf16[1,7424,4]{1,2,0:T(4,128)(2,1)} %param.17) | copy-start | bytes 178180
  19.3 83.5 %copy-start.9 = (bf16[1,8192,4]{1,2,0:T(4,128)(2,1)S(1)}, bf16[1,8192,4]{1,2,0:T(4,128)(2,1)}, u32[]{:S(2)}) copy-start(bf16[1,8192,4]{1,2,0:T(4,128)(2,1)} %param.18) | copy-start | bytes 196612
  19.3 83.6 %copy-start.10 = (bf16[1,7424,4]{1,2,0:T(4,128)(2,1)S(1)}, bf16[1,7424,4]{1,2,0:T(4,128)(2,1)}, u32[]{:S(2)}) copy-start(bf16[1,7424,4]{1,2,0:T(4,128)(2,1)} %param.19) | copy-start | bytes 178180
  105.3 109.4 %all-reduce.5.cloned.1.call-start = ((), (), s32[]{:S(2)}) async-start(), calls=%async_computation.1 | async-start | bytes 1572864 | tf_op jit(solution)/shard_map/psum | solution.py:87
  161.8 10.8 %copy-start.5 = (bf16[8,1024,4]{1,2,0:T(4,128)(2,1)S(1)}, bf16[8,1024,4]{1,2,0:T(4,128)(2,1)}, u32[]{:S(2)}) copy-start(bf16[8,1024,4]{1,2,0:T(4,128)(2,1)} %param.21) | copy-start | bytes 196612
  164.6 32.4 %copy-start.11 = (u32[32]{0:T(128)S(1)}, u32[32]{0:T(128)}, u32[]{:S(2)}) copy-start(u32[32]{0:T(128)} %constant.49) | copy-start | bytes 388
  164.6 50.1 %copy-start.3 = (bf16[24,8192]{1,0:T(8,128)(2,1)S(1)}, bf16[24,8192]{1,0:T(8,128)(2,1)}, u32[]{:S(2)}) copy-start(bf16[24,8192]{1,0:T(8,128)(2,1)} %param.12) | copy-start | bytes 1179652
  164.6 55.1 %copy-start.7 = (s32[24]{0:T(128)S(1)}, s32[24]{0:T(128)}, u32[]{:S(2)}) copy-start(s32[24]{0:T(128)} %param.23) | copy-start | bytes 292
  164.6 81.7 %copy-start.8 = (bf16[8,7424,4]{1,2,0:T(4,128)(2,1)S(1)}, bf16[8,7424,4]{1,2,0:T(4,128)(2,1)}, u32[]{:S(2)}) copy-start(bf16[8,7424,4]{1,2,0:T(4,128)(2,1)} %param.20) | copy-start | bytes 1425412
  254.3 21.0 %copy-start.1 = (bf16[4096,128]{1,0:T(8,128)(2,1)S(1)}, bf16[4096,128]{1,0:T(8,128)(2,1)}, u32[]{:S(2)}) copy-start(bf16[4096,128]{1,0:T(8,128)(2,1)} %param.22) | copy-start | bytes 3145732
Sparse Core Ops, SparseCore 0:
  105.4 56.3 all-gather.2
  197.1 17.4 all-reduce.4
where the time goes:
time: 283 us; the launch traced here: 282 us
  blocking collectives  129 us (46%)
  waiting for transfers between devices  73.5 us (26%)
  matrix products  32.3 us (11%)
  local copies, waits for them, and re-layouts  25.4 us (9%)
  between operations  16.2 us (6%)
  other arithmetic  5.78 us (2%)
    psum x1, blocking collectives, body(): total_gate, total_up = lax.psum((part_gate, part_up), 'pop')  80.8 us
    all_gather x1, waiting for transfers between devices, body(): hidden_portion = lax.all_gather(hidden_state, 'pop', axis=0, tiled=True)  56.4 us
    unnamed x29, local copies, waits for them, and re-layouts  24.8 us
    all_to_all x1, blocking collectives, body(): lax.all_to_all(partial_rows, 'pop', split_axis=0, concat_axis=2, tiled=True)  22.9 us
    unnamed x1, blocking collectives  21.8 us
    psum x1, waiting for transfers between devices, body(): summed = lax.psum(rows_here, 'tensor')[0]  17 us
    dot_general x1, matrix products, body(): jnp.einsum('mfk,mdk->fd', down_input_factors, weighted, preferred_element...  7.97 us
    dot_general x1, matrix products, body(): jnp.einsum('uaz,zh->uah', hidden_portion, down_weight_matrix, preferred_e...  7.93 us
  transfers between devices with their start and end apart: 2, of which 2 were waited for; matrix products, arithmetic and copies ran while one was open for 0% of the time, Pallas kernels for 0%

commit v1 on v0

--- a/solution.py
+++ b/solution.py
@@ -1,8 +1,11 @@
+import functools
 import math
 
 import jax
 import jax.numpy as jnp
 from jax import lax
+from jax.experimental import pallas as pl
+from jax.experimental.pallas import tpu as pltpu
 from jax.sharding import PartitionSpec as P
 
 noise_scale = 0.2
@@ -103,6 +106,395 @@
     return (update.astype(jnp.bfloat16), own_score)
 
 
+BF = jnp.bfloat16
+F32 = jnp.float32
+HI = lax.Precision.HIGHEST
+NT = (((1,), (1,)), ((), ()))
+TN = (((0,), (0,)), ((), ()))
+
+
+def pair_kernel(
+    pop, total_ff,
+    prompts, gate_w, up_w, down_w, gate_in, gof, up_in, uof, dif, dout, head, targets,
+    weighted_out, score_out,
+    wg, wu, dw, normed, fbuild, fac, low, part, ysum, ysend, yrecv, zsend, zrecv, base,
+    lhs_g, lhs_u, hid, acc, lowd, difb, xsend, xrecv, hloc, hrem, hsel,
+    lsend, lrecv, csend, crecv, rbuf,
+    wsem, dsem, hsem, ssem, rsem,
+):
+    rows, width = prompts.shape
+    block, ff = gate_w.shape
+    outer = pop // 2
+    chunk = wg.shape[2]
+    members = pop
+    rank = gof.shape[0]
+    half = block // 2
+    labels = head.shape[1]
+    over = pop * chunk - ff
+    me = lax.axis_index("pop")
+    core = lax.axis_index("tensor")
+    z = me // 2
+    y = me % 2
+    sib = {"tensor": 1 - core}
+
+    def spot(zz, yy):
+        return zz * 2 + yy
+
+    def start_of(c):
+        return pl.multiple_of(c * chunk - (c // (pop - 1)) * over, 128)
+
+    def remote(src, dst, idx, dev):
+        return pltpu.make_async_remote_copy(
+            src_ref=src, dst_ref=dst, send_sem=ssem.at[idx], recv_sem=rsem.at[idx],
+            device_id=dev, device_id_type=pl.DeviceIdType.MESH,
+        )
+
+    owners = [spot((z + 1 + i % outer) % outer, (1 - y) if i < outer else y) for i in range(pop)]
+    loads = []
+    for i in range(pop):
+        cols = pl.ds(start_of(owners[i]), chunk)
+        a = pltpu.make_async_copy(gate_w.at[:, cols], wg.at[i], wsem.at[2 * i])
+        b = pltpu.make_async_copy(up_w.at[:, cols], wu.at[i], wsem.at[2 * i + 1])
+        a.start()
+        b.start()
+        loads.append((a, b))
+    hoff = (me % (pop // 2)) * block
+    hcopy = pltpu.make_async_copy(head.at[pl.ds(pl.multiple_of(hoff + core * half, half), half)], hloc, hsem)
+    hcopy.start()
+
+    barrier = pltpu.get_barrier_semaphore()
+    for k in range(1, pop):
+        pl.semaphore_signal(barrier, inc=1, device_id={"pop": (me + k) % pop}, device_id_type=pl.DeviceIdType.MESH)
+    pl.semaphore_signal(barrier, inc=1, device_id=sib, device_id_type=pl.DeviceIdType.MESH)
+
+    fbuild[0:rank, :] = gof[...].astype(F32)
+    fbuild[rank : 2 * rank, :] = uof[...].astype(F32)
+    fac[me] = fbuild[...].astype(BF)
+    pl.semaphore_wait(barrier, pop)
+
+    pending = []
+    FAC, LOWI, YI, ZI, AGI, XI, HEADI, LI, CI, RI = 0, 8, 16, 20, 24, 32, 33, 34, 42, 43
+    fcopies = {}
+    for k in range(1, outer):
+        d = remote(fac.at[me], fac.at[me], FAC + k, {"pop": spot((z + k) % outer, y)})
+        d.start()
+        fcopies[k] = d
+        pending.append(d)
+    d = remote(fac.at[me], fac.at[me], FAC + outer, {"pop": spot(z, 1 - y)})
+    d.start()
+    fcopies[outer] = d
+    pending.append(d)
+    hs = remote(
+        head.at[pl.ds(pl.multiple_of(hoff + (1 - core) * half, half), half)], hrem, HEADI, sib
+    )
+    hs.start()
+    pending.append(hs)
+
+    x = prompts[...].astype(F32)
+    normed[...] = (x * lax.rsqrt(jnp.mean(x * x, axis=-1, keepdims=True) + norm_eps)).astype(BF)
+
+    scale = noise_scale / math.sqrt(width)
+    lg = (scale * lax.dot_general(normed[...], gate_in[...], NT, preferred_element_type=F32)).astype(BF)
+    lu = (scale * lax.dot_general(normed[...], up_in[...], NT, preferred_element_type=F32)).astype(BF)
+    krow = lax.broadcasted_iota(jnp.int32, (rank, 128), 0)
+    lane = lax.broadcasted_iota(jnp.int32, (rank, 128), 1)
+    sel_g = (lane == me * 2 * rank + krow).astype(F32).astype(BF)
+    sel_u = (lane == me * 2 * rank + rank + krow).astype(F32).astype(BF)
+    low[me] = (
+        jnp.dot(lg, sel_g, preferred_element_type=F32) + jnp.dot(lu, sel_u, preferred_element_type=F32)
+    ).astype(BF)
+    lcopies = []
+    for k in range(1, pop):
+        d = remote(low.at[me], low.at[me], LOWI + k, {"pop": (me + k) % pop})
+        d.start()
+        lcopies.append(d)
+        pending.append(d)
+
+    ycopies = []
+    zcopies = []
+    dloads = []
+    xcols = pl.ds(pl.multiple_of(me * block, block), block)
+    tile = 256
+    for i in range(pop):
+        loads[i][0].wait()
+        loads[i][1].wait()
+        j = i % outer
+        if i >= outer:
+            ycopies[j].wait_recv()
+
+        @pl.loop(0, chunk // tile)
+        def _(s, i=i, j=j):
+            at = pl.ds(pl.multiple_of(s * tile, tile), tile)
+            for g, w in enumerate((wg, wu)):
+                got = jnp.dot(normed[:, xcols], w[i, :, at], preferred_element_type=F32)
+                if i < outer:
+                    ysend[j, g, :, at] = got.astype(BF)
+                elif i < pop - 1:
+                    zsend[j, g, :, at] = (got + yrecv[j, g, :, at].astype(F32)).astype(BF)
+                else:
+                    ysum[g, :, at] = got + yrecv[j, g, :, at].astype(F32)
+
+        if i < outer:
+            d = remote(ysend.at[j], yrecv.at[j], YI + j, {"pop": spot(z, 1 - y)})
+            d.start()
+            ycopies.append(d)
+            pending.append(d)
+        elif i < pop - 1:
+            d = remote(zsend.at[j], zrecv.at[j], ZI + j, {"pop": spot((z + 1 + j) % outer, y)})
+            d.start()
+            zcopies.append(d)
+            pending.append(d)
+        if i == 1:
+            for k in range(1, outer):
+                fcopies[k].wait_recv()
+                src = spot((z + outer - k) % outer, y)
+                d = remote(fac.at[src], fac.at[src], FAC + outer + k, {"pop": spot(z, 1 - y)})
+                d.start()
+                fcopies[outer + k] = d
+                pending.append(d)
+        if i >= outer:
+            step = ff // 4
+            n = i - outer
+            d = pltpu.make_async_copy(
+                down_w.at[pl.ds(n * step, step)], dw.at[pl.ds(n * step, step)], dsem.at[n]
+            )
+            d.start()
+            dloads.append(d)
+
+    total = [ysum[0], ysum[1]]
+    for j in range(outer - 1):
+        zcopies[j].wait_recv()
+        for g in range(2):
+            total[g] = total[g] + zrecv[j, g].astype(F32)
+    for g in range(2):
+        base[0, g] = total[g].astype(BF)
+
+    acopies = {}
+    d = remote(base.at[0], base.at[outer], AGI + outer, {"pop": spot(z, 1 - y)})
+    d.start()
+    acopies[outer] = d
+    pending.append(d)
+    for k in (2, 1, 3):
+        d = remote(base.at[0], base.at[k], AGI + k, {"pop": spot((z + k) % outer, y)})
+        d.start()
+        acopies[k] = d
+        pending.append(d)
+
+    for d in lcopies:
+        d.wait_recv()
+    for k in range(outer, pop):
+        fcopies[k].wait_recv()
+    lhs = jnp.concatenate([low[m].astype(F32) for m in range(members)], axis=0)
+    lanes = lax.broadcasted_iota(jnp.int32, lhs.shape, 1) % (2 * rank)
+    lhs_g[...] = jnp.where(lanes < rank, lhs, 0.0).astype(BF)
+    lhs_u[...] = jnp.where(lanes >= rank, lhs, 0.0).astype(BF)
+    kk = 2 * rank * members
+    for m in range(members):
+        difb[m * rank : (m + 1) * rank, :] = dif[m].astype(F32)
+    acc[...] = jnp.zeros_like(acc)
+    lowd[...] = jnp.zeros_like(lowd)
+
+    def expand(slot, c):
+        start = start_of(c)
+        skip = (c // (pop - 1)) * over
+
+        @pl.loop(0, chunk // tile)
+        def _(s):
+            off = pl.multiple_of(s * tile, tile)
+            at = pl.ds(pl.multiple_of(start + off, 128), tile)
+            f = jnp.concatenate([fac[m, :, at].astype(F32) for m in range(members)], axis=0).astype(BF)
+            gate = jnp.dot(lhs_g[:, :kk], f, preferred_element_type=F32)
+            up = jnp.dot(lhs_u[:, :kk], f, preferred_element_type=F32)
+            bg = base[slot, 0, :, pl.ds(off, tile)].astype(F32)
+            bu = base[slot, 1, :, pl.ds(off, tile)].astype(F32)
+            gate = gate + jnp.concatenate([bg] * members, axis=0)
+            up = up + jnp.concatenate([bu] * members, axis=0)
+            h = gate * (0.5 + 0.5 * jnp.tanh(0.5 * gate)) * up
+            col = lax.broadcasted_iota(jnp.int32, h.shape, 1) + off
+            hid[:, pl.ds(off, tile)] = jnp.where(col >= skip, h, 0.0).astype(BF)
+
+        lowd[...] += lax.dot_general(
+            hid[...], difb[:, pl.ds(start, chunk)].astype(BF), NT, preferred_element_type=F32
+        )
+
+        @pl.loop(0, block // tile)
+        def _(s):
+            at = pl.ds(pl.multiple_of(s * tile, tile), tile)
+            acc[:, at] += jnp.dot(hid[...], dw[pl.ds(start, chunk), at], preferred_element_type=F32)
+
+    for d in dloads:
+        d.wait()
+    expand(0, me)
+    acopies[outer].wait_recv()
+    expand(outer, spot(z, 1 - y))
+    for k in (1, 2, 3):
+        acopies[k].wait_recv()
+        d = remote(base.at[k], base.at[outer + k], AGI + outer + k, {"pop": spot(z, 1 - y)})
+        d.start()
+        acopies[outer + k] = d
+        pending.append(d)
+        expand(k, spot((z + outer - k) % outer, y))
+    for k in (1, 2, 3):
+        acopies[outer + k].wait_recv()
+        expand(outer + k, spot((z + outer - k) % outer, 1 - y))
+
+    mine = lax.broadcasted_iota(jnp.int32, lowd.shape, 0) // rows == lax.broadcasted_iota(jnp.int32, lowd.shape, 1) // rank
+    lowm = jnp.where(mine, lowd[...] * (noise_scale / math.sqrt(total_ff)), 0.0)
+    for m in range(members):
+        fbuild[0:rank, 0:block] = dout[m].astype(F32)
+        weighted_out[m * rank : (m + 1) * rank, :] = fbuild[0:rank, 0:block]
+    acc[...] += jnp.dot(lowm, weighted_out[...], preferred_element_type=F32, precision=HI)
+
+    theirs = pl.ds(pl.multiple_of((1 - core) * half, half), half)
+    ours = pl.ds(pl.multiple_of(core * half, half), half)
+    xsend[...] = acc[:, theirs]
+    xc = remote(xsend, xrecv, XI, sib)
+    xc.start()
+    pending.append(xc)
+    hcopy.wait()
+    hs.wait_recv()
+
+    @pl.when(core == me // (pop // 2))
+    def _():
+        hsel[...] = hloc[...]
+
+    @pl.when(core != me // (pop // 2))
+    def _():
+        hsel[...] = hrem[...]
+
+    pcols = prompts[:, pl.ds(pl.multiple_of(me * block + core * half, half), half)].astype(F32)
+    xc.wait_recv()
+    lsend[...] = jnp.zeros_like(lsend)
+    ones = jnp.ones((8, half), F32)
+    out = acc[:, ours] + xrecv[...] + jnp.concatenate([pcols] * members, axis=0)
+    top = out.astype(BF)
+    rest = (out - top.astype(F32)).astype(BF)
+    logits = jnp.dot(top, hsel[...], preferred_element_type=F32) + jnp.dot(
+        rest, hsel[...], preferred_element_type=F32
+    )
+    squares = out * out
+    for m in range(members):
+        r = slice(m * rows, (m + 1) * rows)
+        lsend[m, 0:rows, :] = logits[r]
+        lsend[m, rows : rows + 8, 0:rows] = lax.dot_general(
+            ones, squares[r], NT, preferred_element_type=F32, precision=HI
+        )
+    bcopies = []
+    for k in range(1, pop):
+        to = (me + k) % pop
+        d = remote(lsend.at[to], lrecv.at[k], LI + k, {"pop": to})
+        d.start()
+        bcopies.append(d)
+        pending.append(d)
+    tot = lsend[me]
+    for k in range(1, pop):
+        bcopies[k - 1].wait_recv()
+        tot = tot + lrecv[k]
+    csend[...] = tot
+    cc = remote(csend, crecv, CI, sib)
+    cc.start()
+    pending.append(cc)
+    cc.wait_recv()
+    tot = csend[...] + crecv[...]
+    eye = (
+        lax.broadcasted_iota(jnp.int32, (rows, labels), 0) == lax.broadcasted_iota(jnp.int32, (rows, labels), 1)
+    ).astype(F32)
+    ssq = jnp.sum(eye * tot[rows : rows + 1, :], axis=1, keepdims=True)
+    lgt = tot[0:rows, :] * lax.rsqrt(ssq * (1.0 / width) + norm_eps)
+    picks = targets[...] == lax.broadcasted_iota(jnp.int32, (rows, labels), 1)
+    picked = jnp.sum(jnp.where(picks, lgt, 0.0), axis=1, keepdims=True)
+    term = picked - jnp.log(jnp.sum(jnp.exp(lgt), axis=1, keepdims=True))
+    reward = jnp.sum(jnp.broadcast_to(term, (rows, 128)), axis=0, keepdims=True) * (1.0 / rows)
+    rbuf[me] = jnp.broadcast_to(reward, (8, 128))
+    rcopies = []
+    for k in range(1, pop):
+        d = remote(rbuf.at[me], rbuf.at[me], RI + k, {"pop": (me + k) % pop})
+        d.start()
+        rcopies.append(d)
+        pending.append(d)
+    for d in rcopies:
+        d.wait_recv()
+    centre = sum(rbuf[m] for m in range(members)) * (1.0 / members)
+    spread = sum((rbuf[m] - centre) * (rbuf[m] - centre) for m in range(members)) * (1.0 / members)
+    inv = lax.rsqrt(spread + norm_eps)
+    score_out[...] = (rbuf[me] - centre) * inv
+    for m in range(members):
+        sc = ((rbuf[m] - centre) * inv)[0:1, 0:1]
+        r = slice(m * rank, (m + 1) * rank)
+        weighted_out[r, :] = (dout[m].astype(F32) * sc).astype(BF).astype(F32)
+    for d in pending:
+        d.wait_send()
+
+
+def update_kernel(norm, dif, weighted, out):
+    members = dif.shape[0]
+    left = jnp.concatenate([dif[m].astype(F32) for m in range(members)], axis=0).astype(BF)
+    got = lax.dot_general(left, weighted[...].astype(BF), TN, preferred_element_type=F32)
+    out[...] = (got * norm).astype(BF)
+
+
+def fast_body(
+    pop, prompts, gate_weight, up_weight, down_weight, gate_in, gof, up_in, uof, dif, dout, head, targets
+):
+    rows, width = prompts.shape
+    block, ff = gate_weight.shape
+    members, _, rank = dif.shape
+    outer = pop // 2
+    chunk = -(-(ff // 128) // pop) * 128
+    labels = head.shape[1]
+    swap = lambda v: jnp.swapaxes(v, 1, 2)
+    dif_t, dout_t = swap(dif), swap(dout)
+    vm = pl.BlockSpec(memory_space=pltpu.VMEM)
+    hb = pl.BlockSpec(memory_space=pl.ANY)
+    V = pltpu.VMEM
+    big = members * rows
+    weighted, score = pl.pallas_call(
+        functools.partial(pair_kernel, pop, 2 * ff),
+        out_shape=(
+            jax.ShapeDtypeStruct((members * rank, block), F32),
+            jax.ShapeDtypeStruct((8, 128), F32),
+        ),
+        in_specs=[vm, hb, hb, hb, vm, vm, vm, vm, vm, vm, hb, vm],
+        out_specs=(vm, vm),
+        scratch_shapes=[
+            V((pop, block, chunk), BF), V((pop, block, chunk), BF), V((ff, block), BF),
+            V((rows, width), BF), V((2 * rank, ff), F32), V((members, 2 * rank, ff), BF),
+            V((members, rows, 128), BF), V((8, 128), F32), V((2, rows, chunk), F32),
+            V((outer, 2, rows, chunk), BF), V((outer, 2, rows, chunk), BF),
+            V((outer, 2, rows, chunk), BF), V((outer, 2, rows, chunk), BF),
+            V((pop, 2, rows, chunk), BF),
+            V((big, 128), BF), V((big, 128), BF), V((big, chunk), BF), V((big, block), F32),
+            V((big, members * rank), F32), V((members * rank, ff), F32),
+            V((big, block // 2), F32), V((big, block // 2), F32),
+            V((block // 2, labels), BF), V((block // 2, labels), BF), V((block // 2, labels), BF),
+            V((members, rows + 8, labels), F32), V((members, rows + 8, labels), F32),
+            V((rows + 8, labels), F32), V((rows + 8, labels), F32), V((members, 8, 128), F32),
+            pltpu.SemaphoreType.DMA((2 * pop,)), pltpu.SemaphoreType.DMA((4,)), pltpu.SemaphoreType.DMA,
+            pltpu.SemaphoreType.DMA((52,)), pltpu.SemaphoreType.DMA((52,)),
+        ],
+        compiler_params=pltpu.CompilerParams(
+            collective_id=0, has_side_effects=True, vmem_limit_bytes=66 * 1000 * 1000
+        ),
+        name="pair",
+    )(
+        prompts, gate_weight, up_weight, down_weight, swap(gate_in)[0], swap(gof)[0], swap(up_in)[0],
+        swap(uof)[0], dif_t, dout_t, head, targets[:, None],
+    )
+    tile = 256
+    update = pl.pallas_call(
+        functools.partial(update_kernel, 1.0 / math.sqrt(members * rank)),
+        grid=(ff // tile,),
+        out_shape=jax.ShapeDtypeStruct((ff, block), BF),
+        in_specs=[
+            pl.BlockSpec((members, rank, tile), lambda i: (0, 0, i)),
+            pl.BlockSpec((members * rank, block), lambda i: (0, 0)),
+        ],
+        out_specs=pl.BlockSpec((tile, block), lambda i: (i, 0)),
+        name="update",
+    )(dif_t, weighted)
+    return update, score[0, :1]
+
+
 def solution(mesh):
     placed = (
         P("groups", None),
@@ -118,8 +510,10 @@
         P("tensor", None),
         P("groups"),
     )
+    pop = mesh.shape["pop"]
+    run = functools.partial(fast_body, pop) if pop == 8 and mesh.shape["tensor"] == 2 else body
     return jax.shard_map(
-        body,
+        run,
         mesh=mesh,
         in_specs=placed,
         out_specs=(P(("groups", "tensor"), "pop"), P(("groups", "pop"))),

time: 283 us -> 93 us (0.33)
  blocking collectives: 129 us -> 0 us
  Pallas kernels: 0 us -> 88 us
  waiting for transfers between devices: 73.5 us -> 0 us
  matrix products: 32.3 us -> 0 us
  local copies, waits for them, and re-layouts: 25.4 us -> 2.53 us
  between operations: 16.2 us -> 0.64 us
  other arithmetic: 5.78 us -> 0 us
    pallas_call x0 -> x2, Pallas kernels: none -> 88 us  [the longest x1 68.9 us: fast_body(): pl.pallas_call(functools.partial(pair_kernel, pop, 2 * ff), out_shape=(ja...]
    psum x2 -> x0, blocking collectives: 84.1 us -> none  [the longest x1 80.8 us: body(): total_gate, total_up = lax.psum((part_gate, part_up), 'pop')]
    all_gather x1 -> x0, waiting for transfers between devices: 56.4 us -> none  [body(): hidden_portion = lax.all_gather(hidden_state, 'pop', axis=0, tiled=True)]
    dot_general x9 -> x0, matrix products: 32.3 us -> none  [the longest x1 7.97 us: body(): jnp.einsum('mfk,mdk->fd', down_input_factors, weighted, preferred_element...]
    unnamed x29 -> x0, local copies, waits for them, and re-layouts: 24.8 us -> none
    all_to_all x1 -> x0, blocking collectives: 22.9 us -> none  [body(): lax.all_to_all(partial_rows, 'pop', split_axis=0, concat_axis=2, tiled=True)]
    unnamed x1 -> x0, blocking collectives: 21.8 us -> none
    psum x1 -> x0, waiting for transfers between devices: 17 us -> none  [body(): summed = lax.psum(rows_here, 'tensor')[0]]
  transfers between devices with their start and end apart: 2 -> 0, of which waited for: 2 -> 0; matrix products, arithmetic and copies ran while one was open for 0% -> 0% of each run, Pallas kernels for 0% -> 0%
where the time goes in v1:
time: 93 us; the launch traced here: 91.2 us
  Pallas kernels  88 us (95%)
  local copies, waits for them, and re-layouts  2.53 us (3%)
    pallas_call x1, Pallas kernels, fast_body(): pl.pallas_call(functools.partial(pair_kernel, pop, 2 * ff), out_shape=(ja...  68.9 us
    pallas_call x1, Pallas kernels, fast_body(): pl.pallas_call(functools.partial(update_kernel, 1.0 / math.sqrt(members *...  19.1 us

profile of v1, /device:TPU:0, one launch (start us, length us, event | category | flops | bytes accessed | tf_op | source)
XLA Modules:
  0.0 91.2 jit_solution(10255078676586098668)
XLA Ops:
  0.6 1.3 %copy.14.targets = s32[24,1]{1,0:T(8,128)} copy(s32[24,1]{0,1:T(1,128)} %bitcast.23) | data formatting | bytes 192 | tf_op jit(solution)/shard_map/broadcast_in_dim | solution.py:481
  2.0 68.9 %pair.1 = (f32[32,1024]{1,0:T(8,128)}, f32[8,128]{1,0:T(8,128)}) custom-call(bf16[24,8192]{1,0:T(8,128)(2,1)} %prompts.1, bf16[1024,7424]{1,0:T(8,128)(2,1)} %gate_w.1, bf16[1024,7424]{1,0:T(8,128)(2,1)} %up_w.1, bf16[7424,1024]{1,0:T(8,128)(2,1)} %down_w.1, bf16[4,8192]{1,0:T(4,128)(2,1)} %bitcast.18, bf16[4,7424]{1,0:T(4,128)(2,1)} %bitcast.21, ...), custom_call_target="tpu_custom_call" | custom-call | tf_op jit(solution)/shard_map/pair/pallas_call | solution.py:451
  70.9 1.2 %slice.3 = f32[1,1]{1,0:T(1,128)} slice(f32[8,128]{1,0:T(8,128)} %get-tuple-element.5), slice={[0:1], [0:1]} | slice | bytes 8 | tf_op jit(solution)/shard_map/slice | solution.py:495
  72.1 19.1 %update.1 = bf16[7424,1024]{1,0:T(8,128)(2,1)} custom-call(bf16[8,4,7424]{2,1,0:T(4,128)(2,1)} %bitcast.17, f32[32,1024]{1,0:T(8,128)} %get-tuple-element.4.weighted), custom_call_target="tpu_custom_call" | custom-call | tf_op jit(solution)/shard_map/update/pallas_call | solution.py:484

commit v2 on v1

--- a/solution.py
+++ b/solution.py
@@ -116,10 +116,10 @@
 def pair_kernel(
     pop, total_ff,
     prompts, gate_w, up_w, down_w, gate_in, gof, up_in, uof, dif, dout, head, targets,
-    weighted_out, score_out,
+    weighted_out, score_out, left_out,
     wg, wu, dw, normed, fbuild, fac, low, part, ysum, ysend, yrecv, zsend, zrecv, base,
     lhs_g, lhs_u, hid, acc, lowd, difb, xsend, xrecv, hloc, hrem, hsel,
-    lsend, lrecv, csend, crecv, rbuf,
+    lsend, lrecv, csend, crecv, rbuf, leftv,
     wsem, dsem, hsem, ssem, rsem,
 ):
     rows, width = prompts.shape
@@ -159,7 +159,7 @@
         b.start()
         loads.append((a, b))
     hoff = (me % (pop // 2)) * block
-    hcopy = pltpu.make_async_copy(head.at[pl.ds(pl.multiple_of(hoff + core * half, half), half)], hloc, hsem)
+    hcopy = pltpu.make_async_copy(head.at[pl.ds(pl.multiple_of(hoff + core * half, half), half)], hloc, hsem.at[0])
     hcopy.start()
 
     barrier = pltpu.get_barrier_semaphore()
@@ -180,10 +180,6 @@
         d.start()
         fcopies[k] = d
         pending.append(d)
-    d = remote(fac.at[me], fac.at[me], FAC + outer, {"pop": spot(z, 1 - y)})
-    d.start()
-    fcopies[outer] = d
-    pending.append(d)
     hs = remote(
         head.at[pl.ds(pl.multiple_of(hoff + (1 - core) * half, half), half)], hrem, HEADI, sib
     )
@@ -244,14 +240,11 @@
             d.start()
             zcopies.append(d)
             pending.append(d)
-        if i == 1:
-            for k in range(1, outer):
-                fcopies[k].wait_recv()
-                src = spot((z + outer - k) % outer, y)
-                d = remote(fac.at[src], fac.at[src], FAC + outer + k, {"pop": spot(z, 1 - y)})
-                d.start()
-                fcopies[outer + k] = d
-                pending.append(d)
+        if i == outer - 1:
+            d = remote(fac.at[me], fac.at[me], FAC + outer, {"pop": spot(z, 1 - y)})
+            d.start()
+            fcopies[outer] = d
+            pending.append(d)
         if i >= outer:
             step = ff // 4
             n = i - outer
@@ -261,6 +254,35 @@
             d.start()
             dloads.append(d)
 
+    for k in range(1, outer):
+        fcopies[k].wait_recv()
+        src = spot((z + outer - k) % outer, y)
+        d = remote(fac.at[src], fac.at[src], FAC + outer + k, {"pop": spot(z, 1 - y)})
+        d.start()
+        fcopies[outer + k] = d
+        pending.append(d)
+
+    for m in range(members):
+        difb[m * rank : (m + 1) * rank, :] = dif[m].astype(F32)
+
+    @pl.loop(0, ff // 128)
+    def _(s):
+        at = pl.ds(pl.multiple_of(s * 128, 128), 128)
+        leftv[at, :] = difb[:, at].T.astype(BF)
+
+    lcopy = pltpu.make_async_copy(leftv, left_out, hsem.at[1])
+    lcopy.start()
+    acc[...] = jnp.zeros_like(acc)
+    lowd[...] = jnp.zeros_like(lowd)
+    for d in lcopies:
+        d.wait_recv()
+    lhs = jnp.concatenate([low[m].astype(F32) for m in range(members)], axis=0)
+    lanes = lax.broadcasted_iota(jnp.int32, lhs.shape, 1) % (2 * rank)
+    lhs_g[...] = jnp.where(lanes < rank, lhs, 0.0).astype(BF)
+    lhs_u[...] = jnp.where(lanes >= rank, lhs, 0.0).astype(BF)
+    for d in dloads:
+        d.wait()
+
     total = [ysum[0], ysum[1]]
     for j in range(outer - 1):
         zcopies[j].wait_recv()
@@ -280,19 +302,9 @@
         acopies[k] = d
         pending.append(d)
 
-    for d in lcopies:
-        d.wait_recv()
     for k in range(outer, pop):
         fcopies[k].wait_recv()
-    lhs = jnp.concatenate([low[m].astype(F32) for m in range(members)], axis=0)
-    lanes = lax.broadcasted_iota(jnp.int32, lhs.shape, 1) % (2 * rank)
-    lhs_g[...] = jnp.where(lanes < rank, lhs, 0.0).astype(BF)
-    lhs_u[...] = jnp.where(lanes >= rank, lhs, 0.0).astype(BF)
     kk = 2 * rank * members
-    for m in range(members):
-        difb[m * rank : (m + 1) * rank, :] = dif[m].astype(F32)
-    acc[...] = jnp.zeros_like(acc)
-    lowd[...] = jnp.zeros_like(lowd)
 
     def expand(slot, c):
         start = start_of(c)
@@ -322,8 +334,6 @@
             at = pl.ds(pl.multiple_of(s * tile, tile), tile)
             acc[:, at] += jnp.dot(hid[...], dw[pl.ds(start, chunk), at], preferred_element_type=F32)
 
-    for d in dloads:
-        d.wait()
     expand(0, me)
     acopies[outer].wait_recv()
     expand(outer, spot(z, 1 - y))
@@ -401,7 +411,9 @@
     ).astype(F32)
     ssq = jnp.sum(eye * tot[rows : rows + 1, :], axis=1, keepdims=True)
     lgt = tot[0:rows, :] * lax.rsqrt(ssq * (1.0 / width) + norm_eps)
-    picks = targets[...] == lax.broadcasted_iota(jnp.int32, (rows, labels), 1)
+    spread_t = jnp.where(eye[:, :rows] > 0.0, jnp.broadcast_to(targets[...].astype(F32), (rows, rows)), 0.0)
+    target = jnp.sum(spread_t, axis=1, keepdims=True).astype(jnp.int32)
+    picks = target == lax.broadcasted_iota(jnp.int32, (rows, labels), 1)
     picked = jnp.sum(jnp.where(picks, lgt, 0.0), axis=1, keepdims=True)
     term = picked - jnp.log(jnp.sum(jnp.exp(lgt), axis=1, keepdims=True))
     reward = jnp.sum(jnp.broadcast_to(term, (rows, 128)), axis=0, keepdims=True) * (1.0 / rows)
@@ -424,13 +436,17 @@
         weighted_out[r, :] = (dout[m].astype(F32) * sc).astype(BF).astype(F32)
     for d in pending:
         d.wait_send()
-
-
-def update_kernel(norm, dif, weighted, out):
-    members = dif.shape[0]
-    left = jnp.concatenate([dif[m].astype(F32) for m in range(members)], axis=0).astype(BF)
-    got = lax.dot_general(left, weighted[...].astype(BF), TN, preferred_element_type=F32)
-    out[...] = (got * norm).astype(BF)
+    lcopy.wait()
+
+
+def update_kernel(norm, left, weighted, score, out, score_out):
+    width = weighted.shape[1]
+    rows = left[...]
+    for n in range(width // 256):
+        at = slice(n * 256, (n + 1) * 256)
+        got = jnp.dot(rows, weighted[:, at].astype(BF), preferred_element_type=F32)
+        out[:, at] = (got * norm).astype(BF)
+    score_out[0] = score[0, 0]
 
 
 def fast_body(
@@ -448,14 +464,15 @@
     hb = pl.BlockSpec(memory_space=pl.ANY)
     V = pltpu.VMEM
     big = members * rows
-    weighted, score = pl.pallas_call(
+    weighted, score, left = pl.pallas_call(
         functools.partial(pair_kernel, pop, 2 * ff),
         out_shape=(
             jax.ShapeDtypeStruct((members * rank, block), F32),
             jax.ShapeDtypeStruct((8, 128), F32),
+            jax.ShapeDtypeStruct((ff, members * rank), BF),
         ),
         in_specs=[vm, hb, hb, hb, vm, vm, vm, vm, vm, vm, hb, vm],
-        out_specs=(vm, vm),
+        out_specs=(vm, vm, hb),
         scratch_shapes=[
             V((pop, block, chunk), BF), V((pop, block, chunk), BF), V((ff, block), BF),
             V((rows, width), BF), V((2 * rank, ff), F32), V((members, 2 * rank, ff), BF),
@@ -468,8 +485,8 @@
             V((big, block // 2), F32), V((big, block // 2), F32),
             V((block // 2, labels), BF), V((block // 2, labels), BF), V((block // 2, labels), BF),
             V((members, rows + 8, labels), F32), V((members, rows + 8, labels), F32),
-            V((rows + 8, labels), F32), V((rows + 8, labels), F32), V((members, 8, 128), F32),
-            pltpu.SemaphoreType.DMA((2 * pop,)), pltpu.SemaphoreType.DMA((4,)), pltpu.SemaphoreType.DMA,
+            V((rows + 8, labels), F32), V((rows + 8, labels), F32), V((members, 8, 128), F32), V((ff, members * rank), BF),
+            pltpu.SemaphoreType.DMA((2 * pop,)), pltpu.SemaphoreType.DMA((4,)), pltpu.SemaphoreType.DMA((2,)),
             pltpu.SemaphoreType.DMA((52,)), pltpu.SemaphoreType.DMA((52,)),
         ],
         compiler_params=pltpu.CompilerParams(
@@ -478,21 +495,25 @@
         name="pair",
     )(
         prompts, gate_weight, up_weight, down_weight, swap(gate_in)[0], swap(gof)[0], swap(up_in)[0],
-        swap(uof)[0], dif_t, dout_t, head, targets[:, None],
-    )
-    tile = 256
-    update = pl.pallas_call(
+        swap(uof)[0], dif_t, dout_t, head, targets[None],
+    )
+    tile = ff // 8
+    update, scores = pl.pallas_call(
         functools.partial(update_kernel, 1.0 / math.sqrt(members * rank)),
         grid=(ff // tile,),
-        out_shape=jax.ShapeDtypeStruct((ff, block), BF),
+        out_shape=(jax.ShapeDtypeStruct((ff, block), BF), jax.ShapeDtypeStruct((1,), F32)),
         in_specs=[
-            pl.BlockSpec((members, rank, tile), lambda i: (0, 0, i)),
+            pl.BlockSpec((tile, members * rank), lambda i: (i, 0)),
             pl.BlockSpec((members * rank, block), lambda i: (0, 0)),
+            pl.BlockSpec((8, 128), lambda i: (0, 0)),
         ],
-        out_specs=pl.BlockSpec((tile, block), lambda i: (i, 0)),
+        out_specs=(
+            pl.BlockSpec((tile, block), lambda i: (i, 0)),
+            pl.BlockSpec(memory_space=pltpu.SMEM),
+        ),
         name="update",
-    )(dif_t, weighted)
-    return update, score[0, :1]
+    )(left, weighted, score)
+    return update, scores
 
 
 def solution(mesh):

time: 93 us -> 74.9 us (0.81); the launches traced: 91.2 us -> 74.5 us
  Pallas kernels: 88 us -> 73.9 us
  local copies, waits for them, and re-layouts: 2.53 us -> 0 us
    pallas_call x1, Pallas kernels: 19.1 us -> 9.83 us  [fast_body(): pl.pallas_call(functools.partial(update_kernel, 1.0 / math.sqrt(members *...]
    pallas_call x1, Pallas kernels: 68.9 us -> 64.1 us  [fast_body(): pl.pallas_call(functools.partial(pair_kernel, pop, 2 * ff), out_shape=(ja...]
    broadcast_in_dim x1 -> x0, local copies, waits for them, and re-layouts: 1.33 us -> none  [fast_body(): targets[:, None]]
    slice x1 -> x0, local copies, waits for them, and re-layouts: 1.2 us -> none  [fast_body(): return (update, score[0, :1])]
where the time goes in v2:
time: 74.9 us; the launch traced here: 74.5 us
  Pallas kernels  73.9 us (99%)
    pallas_call x1, Pallas kernels, fast_body(): pl.pallas_call(functools.partial(pair_kernel, pop, 2 * ff), out_shape=(ja...  64.1 us
    pallas_call x1, Pallas kernels, fast_body(): pl.pallas_call(functools.partial(update_kernel, 1.0 / math.sqrt(members *...  9.83 us

profile of v2, /device:TPU:0, one launch (start us, length us, event | category | flops | bytes accessed | tf_op | source)
XLA Modules:
  0.0 74.5 jit_solution(10607488247318844283)
XLA Ops:
  0.6 64.1 %pair.1 = (f32[32,1024]{1,0:T(8,128)}, f32[8,128]{1,0:T(8,128)}, bf16[7424,32]{1,0:T(8,128)(2,1)}) custom-call(bf16[24,8192]{1,0:T(8,128)(2,1)} %prompts.1, bf16[1024,7424]{1,0:T(8,128)(2,1)} %gate_w.1, bf16[1024,7424]{1,0:T(8,128)(2,1)} %up_w.1, bf16[7424,1024]{1,0:T(8,128)(2,1)} %down_w.1, bf16[4,8192]{1,0:T(4,128)(2,1)} %bitcast.16, ...), custom_call_target="tpu_custom_call" | custom-call | tf_op jit(solution)/shard_map/pair/pallas_call | solution.py:467
  64.7 9.8 %update.1 = (bf16[7424,1024]{1,0:T(8,128)(2,1)}, f32[1]{0:T(128)}) custom-call(bf16[7424,32]{1,0:T(8,128)(2,1)} %get-tuple-element.5.left, f32[32,1024]{1,0:T(8,128)} %get-tuple-element.6.weighted, f32[8,128]{1,0:T(8,128)} %get-tuple-element.7.score), custom_call_target="tpu_custom_call" | custom-call | tf_op jit(solution)/shard_map/update/pallas_call | solution.py:501
